TPU v7x, 32 devices: a whole 2x2x4 slice. The times are simulated.
32 devices in a mesh: row: 4 (over y, x), col: 8 (over z, core).
Axes of the slice: x: 2, y: 2, z: 4, core: 2. Of those that a mesh axis runs over, the one named last changes fastest.
Arguments:
- hist_corr: float32 [16384, 16384], P('row', 'col'), may hold values from -1 to 1
- hist_resp: float32 [16384, 16384], P('row', 'col'), may hold values from -1 to 1, as said below
- row_corr: float32 [128, 16384], P(None, 'col'), may hold values from -1 to 1
- row_resp: float32 [128, 16384], P(None, 'col'), may hold values from -1 to 1
Outputs:
- final_corr: float32 [128, 16384], P(None, 'col')
- final_resp: float32 [128, 16384], P(None, 'col')
Inputs may be any that keep to these rules, and one draw needn't show every extreme that they name: hist_resp[s, u] is 0 where u > s and 1 where u == s.
All inputs are finite; a program needn't handle non-finite values.
Results may differ from a plain program's by a relative error of at most 0.00015.
Values sent between devices are 32-bit elements; how exact they have to be, the bound alone decides.
A program may use at most 128 MiB of HBM per device.

v0:
```python
import math
import jax
import jax.numpy as jnp
from jax import lax
from jax.sharding import PartitionSpec as P

HIST = 16384
BLOCKS = 4
step_size = 0.2
heat_reservoir_warmth = 0.6


def turn_rows(values):
    row_count = lax.axis_size("row")
    col_count = lax.axis_size("col")
    my_row = lax.axis_index("row")
    piece_span = values.shape[1] // row_count
    piece = lax.dynamic_slice_in_dim(values, my_row * piece_span, piece_span, 1)
    spread = jnp.broadcast_to(piece[None, None], (col_count, 1) + piece.shape)
    moved = lax.all_to_all(
        lax.all_to_all(spread, "col", split_axis=0, concat_axis=1, tiled=True),
        "row",
        split_axis=1,
        concat_axis=0,
        tiled=True,
    )
    return jnp.transpose(moved, (2, 1, 0, 3)).reshape(piece.shape[0], -1)


def turn_cols(values):
    row_count = lax.axis_size("row")
    col_count = lax.axis_size("col")
    my_col = lax.axis_index("col")
    factor = col_count // row_count
    block_span = values.shape[1] // factor
    piece_span = block_span // col_count
    blocks = values.reshape(values.shape[0], factor, block_span)
    piece = lax.dynamic_slice_in_dim(blocks, my_col * piece_span, piece_span, 2)
    ordered = jnp.transpose(piece, (1, 0, 2))
    spread = jnp.broadcast_to(ordered[None], (row_count,) + ordered.shape)
    moved = lax.all_to_all(
        lax.all_to_all(spread, "row", split_axis=0, concat_axis=1, tiled=True),
        "col",
        split_axis=1,
        concat_axis=0,
        tiled=True,
    )
    return jnp.transpose(moved[:, 0], (1, 0, 2)).reshape(values.shape[0], -1)


def energy_layout(values):
    return turn_rows(values)


def cross_layout(values):
    return turn_cols(values)


def advance(
    autocovariance_curve,
    perturbation_reaction,
    memory_corr,
    memory_resp,
    cross_term,
    norm_enforcing_scalar,
    integration_coefficient,
):
    next_corr = autocovariance_curve + step_size * (
        integration_coefficient * (memory_corr + cross_term)
        - norm_enforcing_scalar * autocovariance_curve
    )
    next_resp = perturbation_reaction + step_size * (
        integration_coefficient * memory_resp - norm_enforcing_scalar * perturbation_reaction
    )
    return (next_corr, next_resp)


def body(hist_corr, hist_resp, row_corr, row_resp):
    highest = lax.Precision.HIGHEST
    integration_coefficient = 1.0 / math.sqrt(HIST)
    autocovariance_curve = row_corr
    perturbation_reaction = row_resp
    for block_index in range(BLOCKS):
        history_integrand = 3.0 * autocovariance_curve * perturbation_reaction
        slope_contribution = 1.5 * autocovariance_curve * autocovariance_curve
        multiplier_terms = jnp.sum(
            history_integrand * autocovariance_curve + slope_contribution * perturbation_reaction,
            axis=1,
        )
        part_cross = lax.dot_general(
            slope_contribution,
            hist_resp,
            (((1,), (1,)), ((), ())),
            precision=highest,
            preferred_element_type=jnp.float32,
        )
        enforcing_scalar_sum = lax.psum(multiplier_terms, "col")
        energy_rows = energy_layout(history_integrand)
        cross_total = lax.psum(part_cross, "col")
        cross_term = cross_layout(cross_total)
        norm_enforcing_scalar = (
            heat_reservoir_warmth + integration_coefficient * enforcing_scalar_sum[:, None]
        )
        part_corr = jnp.dot(
            energy_rows, hist_corr, precision=highest, preferred_element_type=jnp.float32
        )
        part_resp = jnp.dot(
            energy_rows, hist_resp, precision=highest, preferred_element_type=jnp.float32
        )
        memory_corr, memory_resp = lax.psum((part_corr, part_resp), "row")
        autocovariance_curve, perturbation_reaction = advance(
            autocovariance_curve,
            perturbation_reaction,
            memory_corr,
            memory_resp,
            cross_term,
            norm_enforcing_scalar,
            integration_coefficient,
        )
    return (autocovariance_curve, perturbation_reaction)


def solution(mesh):
    in_specs = (P("row", "col"), P("row", "col"), P(None, "col"), P(None, "col"))
    out_specs = (P(None, "col"), P(None, "col"))
    return jax.shard_map(body, mesh=mesh, in_specs=in_specs, out_specs=out_specs, check_vma=False)
```

profile of v0, /device:TPU:0, one launch (start us, length us, event | category | flops | bytes accessed | tf_op | source)
XLA Modules:
  0.0 1180.2 jit_solution(5139241333706496647)
XLA Ops:
  10.2 55.3 %all_to_all.180 = f32[8,1,128,512]{3,2,1,0:T(8,128)} all-to-all(f32[8,1,128,512]{3,2,1,0:T(8,128)S(1)} %broadcast_in_dim.16), channel_id=1, replica_groups=mesh['row'=4,'col'=8] {'col'}, dimensions={0} | all-to-all | bytes 4194304 | tf_op jit(solution)/shard_map/all_to_all | solution.py:21
  70.1 37.2 %fusion = f32[128,4096]{1,0:T(8,128)S(1)} fusion(f32[4096,2048]{1,0:T(8,128)} %param.5, f32[128,2048]{1,0:T(8,128)S(1)} %copy-done.4), kind=kOutput, calls=%fused_computation.20 | convolution fusion | flops 12885426176 | bytes 36700160 | tf_op jit(solution)/shard_map/dot_general | solution.py:90
  110.3 64.6 %all-reduce.13.cloned.1.call-done = f32[128,2,2048]{2,1,0:T(2,128)} async-done(((f32[128,2,2048]{2,1,0:T(2,128)}), f32[128,2,2048]{2,1,0:T(2,128)}) %all-reduce.13.cloned.1.call-update) | async-done | bytes 2097168 | tf_op jit(solution)/shard_map/psum | solution.py:99
  183.6 22.4 %fusion.13 = f32[128,2048]{1,0:T(8,128)} fusion(f32[128,4096]{0,1:T(8,128)S(1)} %bitcast.88, f32[4096,2048]{1,0:T(8,128)} %param.5), kind=kOutput, calls=%fused_computation.45 | convolution fusion | flops 12884901888 | bytes 36700160 | tf_op jit(solution)/shard_map/dot_general | solution.py:107
  234.3 29.3 %psum.114 = f32[128]{0:T(128)S(1)} all-reduce(f32[128]{0:T(128)S(1)} %get-tuple-element.20), channel_id=1, replica_groups=mesh['row'=4,'col'=8] {'col'}, use_global_device_ids=true, to_apply=%region_3.0 | all-reduce | flops 128 | bytes 1024 | tf_op jit(solution)/shard_map/psum | solution.py:97
  264.8 33.0 %all-reduce.27.cloned.1.call-done = (f32[128,2048]{1,0:T(8,128)}, f32[128,2048]{1,0:T(8,128)}) async-done(((f32[128,2048]{1,0:T(8,128)}, f32[128,2048]{1,0:T(8,128)}), (f32[128,2048]{1,0:T(8,128)}, f32[128,2048]{1,0:T(8,128)})) %all-reduce.27.cloned.1.call-update) | async-done | bytes 2097168 | tf_op jit(solution)/shard_map/psum | solution.py:110
  301.2 53.5 %all_to_all.181 = f32[8,1,128,512]{3,2,1,0:T(8,128)} all-to-all(f32[8,1,128,512]{3,2,1,0:T(8,128)S(1)} %broadcast_in_dim.18), channel_id=1, replica_groups=mesh['row'=4,'col'=8] {'col'}, dimensions={0} | all-to-all | bytes 4194304 | tf_op jit(solution)/shard_map/all_to_all | solution.py:21
  359.5 39.0 %fusion.1 = f32[128,4096]{1,0:T(8,128)} fusion(f32[4096,2048]{1,0:T(8,128)} %param.5, f32[128,2048]{1,0:T(8,128)S(1)} %get-tuple-element.18), kind=kOutput, calls=%fused_computation.21 | convolution fusion | flops 12885426176 | bytes 36700160 | tf_op jit(solution)/shard_map/dot_general | solution.py:90
  402.5 64.6 %all-reduce.15.cloned.1.call-done = f32[128,2,2048]{2,1,0:T(2,128)} async-done(((f32[128,2,2048]{2,1,0:T(2,128)}), f32[128,2,2048]{2,1,0:T(2,128)}) %all-reduce.15.cloned.1.call-update) | async-done | bytes 2097168 | tf_op jit(solution)/shard_map/psum | solution.py:99
  476.0 22.4 %fusion.15 = f32[128,2048]{1,0:T(8,128)} fusion(f32[128,4096]{0,1:T(8,128)S(1)} %bitcast.90, f32[4096,2048]{1,0:T(8,128)} %param.5), kind=kOutput, calls=%fused_computation.47 | convolution fusion | flops 12884901888 | bytes 36700160 | tf_op jit(solution)/shard_map/dot_general | solution.py:107
  526.9 29.3 %psum.118 = f32[128]{0:T(128)S(1)} all-reduce(f32[128]{0:T(128)S(1)} %get-tuple-element.16), channel_id=1, replica_groups=mesh['row'=4,'col'=8] {'col'}, use_global_device_ids=true, to_apply=%region_8.0 | all-reduce | flops 128 | bytes 1024 | tf_op jit(solution)/shard_map/psum | solution.py:97
  557.3 32.9 %all-reduce.25.cloned.1.call-done = (f32[128,2048]{1,0:T(8,128)}, f32[128,2048]{1,0:T(8,128)}) async-done(((f32[128,2048]{1,0:T(8,128)}, f32[128,2048]{1,0:T(8,128)}), (f32[128,2048]{1,0:T(8,128)}, f32[128,2048]{1,0:T(8,128)})) %all-reduce.25.cloned.1.call-update) | async-done | bytes 2097168 | tf_op jit(solution)/shard_map/psum | solution.py:110
  593.9 53.5 %all_to_all.182 = f32[8,1,128,512]{3,2,1,0:T(8,128)} all-to-all(f32[8,1,128,512]{3,2,1,0:T(8,128)S(1)} %broadcast_in_dim.20), channel_id=1, replica_groups=mesh['row'=4,'col'=8] {'col'}, dimensions={0} | all-to-all | bytes 4194304 | tf_op jit(solution)/shard_map/all_to_all | solution.py:21
  652.1 37.2 %fusion.2 = f32[128,4096]{1,0:T(8,128)S(1)} fusion(f32[4096,2048]{1,0:T(8,128)} %param.5, f32[128,2048]{1,0:T(8,128)S(1)} %get-tuple-element.15), kind=kOutput, calls=%fused_computation.22 | convolution fusion | flops 12885426176 | bytes 36700160 | tf_op jit(solution)/shard_map/dot_general | solution.py:90
  692.2 64.6 %all-reduce.17.cloned.1.call-done = f32[128,2,2048]{2,1,0:T(2,128)} async-done(((f32[128,2,2048]{2,1,0:T(2,128)}), f32[128,2,2048]{2,1,0:T(2,128)}) %all-reduce.17.cloned.1.call-update) | async-done | bytes 2097168 | tf_op jit(solution)/shard_map/psum | solution.py:99
  765.5 22.4 %fusion.17 = f32[128,2048]{1,0:T(8,128)} fusion(f32[128,4096]{0,1:T(8,128)S(1)} %bitcast.92, f32[4096,2048]{1,0:T(8,128)} %param.5), kind=kOutput, calls=%fused_computation.49 | convolution fusion | flops 12884901888 | bytes 36700160 | tf_op jit(solution)/shard_map/dot_general | solution.py:107
  816.4 29.3 %psum.122 = f32[128]{0:T(128)S(1)} all-reduce(f32[128]{0:T(128)S(1)} %get-tuple-element.13), channel_id=1, replica_groups=mesh['row'=4,'col'=8] {'col'}, use_global_device_ids=true, to_apply=%region_13.0 | all-reduce | flops 128 | bytes 1024 | tf_op jit(solution)/shard_map/psum | solution.py:97
  846.9 32.9 %all-reduce.23.cloned.1.call-done = (f32[128,2048]{1,0:T(8,128)}, f32[128,2048]{1,0:T(8,128)}) async-done(((f32[128,2048]{1,0:T(8,128)}, f32[128,2048]{1,0:T(8,128)}), (f32[128,2048]{1,0:T(8,128)}, f32[128,2048]{1,0:T(8,128)})) %all-reduce.23.cloned.1.call-update) | async-done | bytes 2097168 | tf_op jit(solution)/shard_map/psum | solution.py:110
  883.4 53.5 %all_to_all.183 = f32[8,1,128,512]{3,2,1,0:T(8,128)} all-to-all(f32[8,1,128,512]{3,2,1,0:T(8,128)S(1)} %broadcast_in_dim.22), channel_id=1, replica_groups=mesh['row'=4,'col'=8] {'col'}, dimensions={0} | all-to-all | bytes 4194304 | tf_op jit(solution)/shard_map/all_to_all | solution.py:21
  941.9 37.3 %fusion.3 = f32[128,4096]{1,0:T(8,128)S(1)} fusion(f32[4096,2048]{1,0:T(8,128)} %param.5, f32[128,2048]{1,0:T(8,128)S(1)} %get-tuple-element.12), kind=kOutput, calls=%fused_computation.23 | convolution fusion | flops 12885426176 | bytes 36700160 | tf_op jit(solution)/shard_map/dot_general | solution.py:90
  982.0 64.6 %all-reduce.19.cloned.1.call-done = f32[128,2,2048]{2,1,0:T(2,128)} async-done(((f32[128,2,2048]{2,1,0:T(2,128)}), f32[128,2,2048]{2,1,0:T(2,128)}) %all-reduce.19.cloned.1.call-update) | async-done | bytes 2097168 | tf_op jit(solution)/shard_map/psum | solution.py:99
  1054.6 22.4 %fusion.19 = f32[128,2048]{1,0:T(8,128)} fusion(f32[128,4096]{0,1:T(8,128)S(1)} %bitcast.94, f32[4096,2048]{1,0:T(8,128)} %param.5), kind=kOutput, calls=%fused_computation.51 | convolution fusion | flops 12884901888 | bytes 36700160 | tf_op jit(solution)/shard_map/dot_general | solution.py:107
  1104.3 29.3 %psum.126 = f32[128]{0:T(128)S(1)} all-reduce(f32[128]{0:T(128)S(1)} %get-tuple-element.10), channel_id=1, replica_groups=mesh['row'=4,'col'=8] {'col'}, use_global_device_ids=true, to_apply=%region_18.0 | all-reduce | flops 128 | bytes 1024 | tf_op jit(solution)/shard_map/psum | solution.py:97
  1134.7 34.2 %all-reduce.21.cloned.1.call-done = (f32[128,2048]{1,0:T(8,128)}, f32[128,2048]{1,0:T(8,128)}) async-done(((f32[128,2048]{1,0:T(8,128)}, f32[128,2048]{1,0:T(8,128)}), (f32[128,2048]{1,0:T(8,128)}, f32[128,2048]{1,0:T(8,128)})) %all-reduce.21.cloned.1.call-update) | async-done | bytes 2097168 | tf_op jit(solution)/shard_map/psum | solution.py:110
  (106 shorter events, 198.9 us)
Async XLA Ops:
  65.5 110.4 %all-to-all-start.1 = ((f32[1,8,128,512]{3,2,0,1:T(8,128)}), f32[1,8,128,512]{3,2,0,1:T(8,128)}, u32[]{:S(2)}, u32[]{:S(2)}) async-start(f32[1,8,128,512]{3,2,0,1:T(8,128)} %bitcast.1), calls=%async_computation.1 | async-start | bytes 4194304 | tf_op jit(solution)/shard_map/all_to_all | solution.py:20
  70.1 104.8 %all-reduce.13.cloned.1.call-start = ((), (), s32[]{:S(2)}) async-start(), calls=%async_computation.16 | async-start | bytes 4194304 | tf_op jit(solution)/shard_map/psum | solution.py:99
  177.2 51.3 %all-to-all-start.2 = ((f32[4,2,128,256]{3,1,2,0:T(2,128)}), f32[4,2,128,256]{3,1,2,0:T(2,128)}, u32[]{:S(2)}, u32[]{:S(2)}) async-start(f32[4,2,128,256]{3,1,2,0:T(2,128)} %broadcast_in_dim.17), calls=%async_computation.2 | async-start | bytes 2097152 | tf_op jit(solution)/shard_map/all_to_all | solution.py:42
  181.4 116.4 %all-reduce.27.cloned.1.call-start = ((), (), s32[]{:S(2)}) async-start(), calls=%async_computation.23 | async-start | bytes 4194304 | tf_op jit(solution)/shard_map/psum | solution.py:110
  230.8 32.9 %all-to-all-start.3 = ((f32[1,8,128,256]{3,2,0,1:T(8,128)}), f32[1,8,128,256]{3,2,0,1:T(8,128)S(1)}, u32[]{:S(2)}, u32[]{:S(2)}) async-start(f32[1,8,128,256]{3,2,0,1:T(8,128)} %bitcast.7), calls=%async_computation.3 | async-start | bytes 2097152 | tf_op jit(solution)/shard_map/all_to_all | solution.py:41
  354.8 113.3 %all-to-all-start.5 = ((f32[1,8,128,512]{3,2,0,1:T(8,128)}), f32[1,8,128,512]{3,2,0,1:T(8,128)}, u32[]{:S(2)}, u32[]{:S(2)}) async-start(f32[1,8,128,512]{3,2,0,1:T(8,128)} %bitcast.96), calls=%async_computation.5 | async-start | bytes 4194304 | tf_op jit(solution)/shard_map/all_to_all | solution.py:20
  359.2 107.9 %all-reduce.15.cloned.1.call-start = ((), (), s32[]{:S(2)}) async-start(), calls=%async_computation.17 | async-start | bytes 4194304 | tf_op jit(solution)/shard_map/psum | solution.py:99
  469.3 51.5 %all-to-all-start.6 = ((f32[4,2,128,256]{3,1,2,0:T(2,128)}), f32[4,2,128,256]{3,1,2,0:T(2,128)}, u32[]{:S(2)}, u32[]{:S(2)}) async-start(f32[4,2,128,256]{3,1,2,0:T(2,128)} %broadcast_in_dim.19), calls=%async_computation.6 | async-start | bytes 2097152 | tf_op jit(solution)/shard_map/all_to_all | solution.py:42
  473.6 116.6 %all-reduce.25.cloned.1.call-start = ((), (), s32[]{:S(2)}) async-start(), calls=%async_computation.22 | async-start | bytes 4194304 | tf_op jit(solution)/shard_map/psum | solution.py:110
  523.2 67.0 %copy-start.1 = (f32[128,2048]{1,0:T(8,128)S(1)}, f32[128,2048]{1,0:T(8,128)}, u32[]{:S(2)}) copy-start(f32[128,2048]{1,0:T(8,128)} %copy-done) | copy-start | bytes 3145732
  523.2 33.0 %all-to-all-start.7 = ((f32[1,8,128,256]{3,2,0,1:T(8,128)}), f32[1,8,128,256]{3,2,0,1:T(8,128)S(1)}, u32[]{:S(2)}, u32[]{:S(2)}) async-start(f32[1,8,128,256]{3,2,0,1:T(8,128)} %bitcast.101), calls=%async_computation.7 | async-start | bytes 2097152 | tf_op jit(solution)/shard_map/all_to_all | solution.py:41
  647.4 110.4 %all-to-all-start.9 = ((f32[1,8,128,512]{3,2,0,1:T(8,128)}), f32[1,8,128,512]{3,2,0,1:T(8,128)}, u32[]{:S(2)}, u32[]{:S(2)}) async-start(f32[1,8,128,512]{3,2,0,1:T(8,128)} %bitcast.21), calls=%async_computation.9 | async-start | bytes 4194304 | tf_op jit(solution)/shard_map/all_to_all | solution.py:20
  651.8 105.0 %all-reduce.17.cloned.1.call-start = ((), (), s32[]{:S(2)}) async-start(), calls=%async_computation.18 | async-start | bytes 4194304 | tf_op jit(solution)/shard_map/psum | solution.py:99
  759.1 51.3 %all-to-all-start.10 = ((f32[4,2,128,256]{3,1,2,0:T(2,128)}), f32[4,2,128,256]{3,1,2,0:T(2,128)}, u32[]{:S(2)}, u32[]{:S(2)}) async-start(f32[4,2,128,256]{3,1,2,0:T(2,128)} %broadcast_in_dim.21), calls=%async_computation.10 | async-start | bytes 2097152 | tf_op jit(solution)/shard_map/all_to_all | solution.py:42
  763.3 116.5 %all-reduce.23.cloned.1.call-start = ((), (), s32[]{:S(2)}) async-start(), calls=%async_computation.21 | async-start | bytes 4194304 | tf_op jit(solution)/shard_map/psum | solution.py:110
  812.7 67.0 %copy-start.6 = (f32[128,2048]{1,0:T(8,128)S(1)}, f32[128,2048]{1,0:T(8,128)}, u32[]{:S(2)}) copy-start(f32[128,2048]{1,0:T(8,128)} %copy-done.5) | copy-start | bytes 3145732
  812.7 33.0 %all-to-all-start.11 = ((f32[1,8,128,256]{3,2,0,1:T(8,128)}), f32[1,8,128,256]{3,2,0,1:T(8,128)S(1)}, u32[]{:S(2)}, u32[]{:S(2)}) async-start(f32[1,8,128,256]{3,2,0,1:T(8,128)} %bitcast.102), calls=%async_computation.11 | async-start | bytes 2097152 | tf_op jit(solution)/shard_map/all_to_all | solution.py:41
  936.9 110.6 %all-to-all-start.13 = ((f32[1,8,128,512]{3,2,0,1:T(8,128)}), f32[1,8,128,512]{3,2,0,1:T(8,128)}, u32[]{:S(2)}, u32[]{:S(2)}) async-start(f32[1,8,128,512]{3,2,0,1:T(8,128)} %bitcast.31), calls=%async_computation.13 | async-start | bytes 4194304 | tf_op jit(solution)/shard_map/all_to_all | solution.py:20
  941.4 105.2 %all-reduce.19.cloned.1.call-start = ((), (), s32[]{:S(2)}) async-start(), calls=%async_computation.19 | async-start | bytes 4194304 | tf_op jit(solution)/shard_map/psum | solution.py:99
  1048.8 50.7 %all-to-all-start.14 = ((f32[4,2,128,256]{3,1,2,0:T(2,128)}), f32[4,2,128,256]{3,1,2,0:T(2,128)S(1)}, u32[]{:S(2)}, u32[]{:S(2)}) async-start(f32[4,2,128,256]{3,1,2,0:T(2,128)} %broadcast_in_dim.23), calls=%async_computation.14 | async-start | bytes 2097152 | tf_op jit(solution)/shard_map/all_to_all | solution.py:42
  1052.5 116.5 %all-reduce.21.cloned.1.call-start = ((), (), s32[]{:S(2)}) async-start(), calls=%async_computation.20 | async-start | bytes 4194304 | tf_op jit(solution)/shard_map/psum | solution.py:110
  1100.6 68.4 %copy-start.3 = (f32[128,2048]{1,0:T(8,128)S(1)}, f32[128,2048]{1,0:T(8,128)}, u32[]{:S(2)}) copy-start(f32[128,2048]{1,0:T(8,128)} %copy-done.2) | copy-start | bytes 3145732
  1100.6 68.4 %copy-start.8 = (f32[128,2048]{1,0:T(8,128)S(1)}, f32[128,2048]{1,0:T(8,128)}, u32[]{:S(2)}) copy-start(f32[128,2048]{1,0:T(8,128)} %copy-done.7) | copy-start | bytes 3145732
  1100.6 33.0 %all-to-all-start.15 = ((f32[1,8,128,256]{3,2,0,1:T(8,128)}), f32[1,8,128,256]{3,2,0,1:T(8,128)S(1)}, u32[]{:S(2)}, u32[]{:S(2)}) async-start(f32[1,8,128,256]{3,2,0,1:T(8,128)} %bitcast.103), calls=%async_computation.15 | async-start | bytes 2097152 | tf_op jit(solution)/shard_map/all_to_all | solution.py:41
  (5 other events, 124.7 us)
Sparse Core Ops, SparseCore 0:
  110.4 64.4 all-reduce.12
  402.6 64.4 all-reduce.14
  692.3 64.4 all-reduce.16
  982.1 64.4 all-reduce.18
Sparse Core Ops, SparseCore 1:
  228.5 69.2 all-reduce.26
  521.0 69.2 all-reduce.24
  810.5 69.2 all-reduce.22
  1099.6 69.3 all-reduce.20
where the time goes:
time: 1190 us; the launch traced here: 1180 us
  waiting for transfers between devices  392 us (33%)
  blocking collectives  333 us (28%)
  matrix products  330 us (28%)
  starting transfers between devices  51 us (4%)
  local copies, waits for them, and re-layouts  43.7 us (4%)
  between operations  16.1 us (1%)
  other arithmetic  14.3 us (1%)
    psum x4, waiting for transfers between devices, body(): cross_total = lax.psum(part_cross, 'col')  258 us
    all_to_all x4, blocking collectives, turn_rows(): lax.all_to_all(spread, 'col', split_axis=0, concat_axis=1, tiled=True)  216 us
    dot_general x4, matrix products, body(): lax.dot_general(slope_contribution, hist_resp, (((1,), (1,)), ((), ())),...  151 us
    psum x4, waiting for transfers between devices, body(): memory_corr, memory_resp = lax.psum((part_corr, part_resp), 'row')  133 us
    psum x4, blocking collectives, body(): enforcing_scalar_sum = lax.psum(multiplier_terms, 'col')  117 us
    dot_general x4, matrix products, body(): jnp.dot(energy_rows, hist_resp, precision=highest, preferred_element_type...  89.7 us
    dot_general x4, matrix products, body(): jnp.dot(energy_rows, hist_corr, precision=highest, preferred_element_type...  89.7 us
  transfers between devices with their start and end apart: 20, of which 8 were waited for; matrix products, arithmetic and copies ran while one was open for 31% of the time, Pallas kernels for 0%

commit v1 on v0

--- a/solution.py
+++ b/solution.py
@@ -94,7 +94,8 @@
             precision=highest,
             preferred_element_type=jnp.float32,
         )
-        enforcing_scalar_sum = lax.psum(multiplier_terms, "col")
+        pieces = lax.all_gather(multiplier_terms, "col")
+        enforcing_scalar_sum = jnp.sum(pieces, axis=0)
         energy_rows = energy_layout(history_integrand)
         cross_total = lax.psum(part_cross, "col")
         cross_term = cross_layout(cross_total)

time: 1190 us -> 1190 us (level)
  blocking collectives: 333 us -> 315 us
  waiting for transfers between devices: 392 us -> 410 us
    psum x4 -> x0, blocking collectives: 117 us -> none  [body(): enforcing_scalar_sum = lax.psum(multiplier_terms, 'col')]
    all_gather x0 -> x4, blocking collectives: none -> 98.6 us  [body(): pieces = lax.all_gather(multiplier_terms, 'col')]
  transfers between devices with their start and end apart: 20 -> 20, of which waited for: 8 -> 12; matrix products, arithmetic and copies ran while one was open for 31% -> 31% of each run, Pallas kernels for 0% -> 0%
where the time goes in v1:
time: 1190 us; the launch traced here: 1180 us
  waiting for transfers between devices  410 us (34%)
  matrix products  330 us (28%)
  blocking collectives  315 us (26%)
  starting transfers between devices  51 us (4%)
  local copies, waits for them, and re-layouts  43.7 us (4%)
  between operations  16.1 us (1%)
  other arithmetic  14.4 us (1%)
    psum x4, waiting for transfers between devices, body(): cross_total = lax.psum(part_cross, 'col')  259 us
    all_to_all x4, blocking collectives, turn_rows(): lax.all_to_all(spread, 'col', split_axis=0, concat_axis=1, tiled=True)  216 us
    dot_general x4, matrix products, body(): lax.dot_general(slope_contribution, hist_resp, (((1,), (1,)), ((), ())),...  151 us
    psum x4, waiting for transfers between devices, body(): memory_corr, memory_resp = lax.psum((part_corr, part_resp), 'row')  144 us
    all_gather x4, blocking collectives, body(): pieces = lax.all_gather(multiplier_terms, 'col')  98.6 us
    dot_general x4, matrix products, body(): jnp.dot(energy_rows, hist_resp, precision=highest, preferred_element_type...  89.7 us
    dot_general x4, matrix products, body(): jnp.dot(energy_rows, hist_corr, precision=highest, preferred_element_type...  89.7 us
  transfers between devices with their start and end apart: 20, of which 12 were waited for; matrix products, arithmetic and copies ran while one was open for 31% of the time, Pallas kernels for 0%

profile of v1, /device:TPU:0, one launch (start us, length us, event | category | flops | bytes accessed | tf_op | source)
XLA Modules:
  0.0 1180.3 jit_solution(17961527713946366073)
XLA Ops:
  10.2 55.3 %all_to_all.180 = f32[8,1,128,512]{3,2,1,0:T(8,128)} all-to-all(f32[8,1,128,512]{3,2,1,0:T(8,128)S(1)} %broadcast_in_dim.16), channel_id=1, replica_groups=mesh['row'=4,'col'=8] {'col'}, dimensions={0} | all-to-all | bytes 4194304 | tf_op jit(solution)/shard_map/all_to_all | solution.py:21
  70.1 37.2 %fusion = f32[128,4096]{1,0:T(8,128)S(1)} fusion(f32[4096,2048]{1,0:T(8,128)} %param.5, f32[128,2048]{1,0:T(8,128)S(1)} %copy-done.4), kind=kOutput, calls=%fused_computation.20 | convolution fusion | flops 12885426176 | bytes 36700160 | tf_op jit(solution)/shard_map/dot_general | solution.py:90
  110.3 64.6 %all-reduce.13.cloned.1.call-done = f32[128,2,2048]{2,1,0:T(2,128)} async-done(((f32[128,2,2048]{2,1,0:T(2,128)}), f32[128,2,2048]{2,1,0:T(2,128)}) %all-reduce.13.cloned.1.call-update) | async-done | bytes 2097168 | tf_op jit(solution)/shard_map/psum | solution.py:100
  183.6 22.4 %fusion.13 = f32[128,2048]{1,0:T(8,128)} fusion(f32[128,4096]{0,1:T(8,128)S(1)} %bitcast.92, f32[4096,2048]{1,0:T(8,128)} %param.5), kind=kOutput, calls=%fused_computation.45 | convolution fusion | flops 12884901888 | bytes 36700160 | tf_op jit(solution)/shard_map/dot_general | solution.py:108
  234.3 24.7 %all-gather.4 = f32[8,1,128]{2,1,0:T(1,128)S(1)} all-gather(f32[1,1,128]{2,1,0:T(1,128)S(1)} %bitcast.115), channel_id=2, replica_groups=mesh['row'=4,'col'=8] {'col'}, dimensions={0}, use_global_device_ids=true | all-gather | bytes 4608 | tf_op jit(solution)/shard_map/all_gather | solution.py:97
  261.9 35.9 %all-reduce.27.cloned.1.call-done = (f32[128,2048]{1,0:T(8,128)}, f32[128,2048]{1,0:T(8,128)}) async-done(((f32[128,2048]{1,0:T(8,128)}, f32[128,2048]{1,0:T(8,128)}), (f32[128,2048]{1,0:T(8,128)}, f32[128,2048]{1,0:T(8,128)})) %all-reduce.27.cloned.1.call-update) | async-done | bytes 2097168 | tf_op jit(solution)/shard_map/psum | solution.py:111
  301.2 53.5 %all_to_all.181 = f32[8,1,128,512]{3,2,1,0:T(8,128)} all-to-all(f32[8,1,128,512]{3,2,1,0:T(8,128)S(1)} %broadcast_in_dim.18), channel_id=1, replica_groups=mesh['row'=4,'col'=8] {'col'}, dimensions={0} | all-to-all | bytes 4194304 | tf_op jit(solution)/shard_map/all_to_all | solution.py:21
  359.5 39.0 %fusion.1 = f32[128,4096]{1,0:T(8,128)} fusion(f32[4096,2048]{1,0:T(8,128)} %param.5, f32[128,2048]{1,0:T(8,128)S(1)} %get-tuple-element.18), kind=kOutput, calls=%fused_computation.21 | convolution fusion | flops 12885426176 | bytes 36700160 | tf_op jit(solution)/shard_map/dot_general | solution.py:90
  402.5 64.6 %all-reduce.15.cloned.1.call-done = f32[128,2,2048]{2,1,0:T(2,128)} async-done(((f32[128,2,2048]{2,1,0:T(2,128)}), f32[128,2,2048]{2,1,0:T(2,128)}) %all-reduce.15.cloned.1.call-update) | async-done | bytes 2097168 | tf_op jit(solution)/shard_map/psum | solution.py:100
  476.0 22.4 %fusion.15 = f32[128,2048]{1,0:T(8,128)} fusion(f32[128,4096]{0,1:T(8,128)S(1)} %bitcast.94, f32[4096,2048]{1,0:T(8,128)} %param.5), kind=kOutput, calls=%fused_computation.47 | convolution fusion | flops 12884901888 | bytes 36700160 | tf_op jit(solution)/shard_map/dot_general | solution.py:108
  526.9 24.7 %all-gather.5 = f32[8,1,128]{2,1,0:T(1,128)S(1)} all-gather(f32[1,1,128]{2,1,0:T(1,128)S(1)} %bitcast.114), channel_id=3, replica_groups=mesh['row'=4,'col'=8] {'col'}, dimensions={0}, use_global_device_ids=true | all-gather | bytes 4608 | tf_op jit(solution)/shard_map/all_gather | solution.py:97
  554.5 35.7 %all-reduce.25.cloned.1.call-done = (f32[128,2048]{1,0:T(8,128)}, f32[128,2048]{1,0:T(8,128)}) async-done(((f32[128,2048]{1,0:T(8,128)}, f32[128,2048]{1,0:T(8,128)}), (f32[128,2048]{1,0:T(8,128)}, f32[128,2048]{1,0:T(8,128)})) %all-reduce.25.cloned.1.call-update) | async-done | bytes 2097168 | tf_op jit(solution)/shard_map/psum | solution.py:111
  593.8 53.5 %all_to_all.182 = f32[8,1,128,512]{3,2,1,0:T(8,128)} all-to-all(f32[8,1,128,512]{3,2,1,0:T(8,128)S(1)} %broadcast_in_dim.20), channel_id=1, replica_groups=mesh['row'=4,'col'=8] {'col'}, dimensions={0} | all-to-all | bytes 4194304 | tf_op jit(solution)/shard_map/all_to_all | solution.py:21
  652.1 37.2 %fusion.2 = f32[128,4096]{1,0:T(8,128)S(1)} fusion(f32[4096,2048]{1,0:T(8,128)} %param.5, f32[128,2048]{1,0:T(8,128)S(1)} %get-tuple-element.15), kind=kOutput, calls=%fused_computation.22 | convolution fusion | flops 12885426176 | bytes 36700160 | tf_op jit(solution)/shard_map/dot_general | solution.py:90
  692.2 64.7 %all-reduce.17.cloned.1.call-done = f32[128,2,2048]{2,1,0:T(2,128)} async-done(((f32[128,2,2048]{2,1,0:T(2,128)}), f32[128,2,2048]{2,1,0:T(2,128)}) %all-reduce.17.cloned.1.call-update) | async-done | bytes 2097168 | tf_op jit(solution)/shard_map/psum | solution.py:100
  765.6 22.4 %fusion.17 = f32[128,2048]{1,0:T(8,128)} fusion(f32[128,4096]{0,1:T(8,128)S(1)} %bitcast.96, f32[4096,2048]{1,0:T(8,128)} %param.5), kind=kOutput, calls=%fused_computation.49 | convolution fusion | flops 12884901888 | bytes 36700160 | tf_op jit(solution)/shard_map/dot_general | solution.py:108
  816.5 24.7 %all-gather.6 = f32[8,1,128]{2,1,0:T(1,128)S(1)} all-gather(f32[1,1,128]{2,1,0:T(1,128)S(1)} %bitcast.113), channel_id=4, replica_groups=mesh['row'=4,'col'=8] {'col'}, dimensions={0}, use_global_device_ids=true | all-gather | bytes 4608 | tf_op jit(solution)/shard_map/all_gather | solution.py:97
  844.1 35.7 %all-reduce.23.cloned.1.call-done = (f32[128,2048]{1,0:T(8,128)}, f32[128,2048]{1,0:T(8,128)}) async-done(((f32[128,2048]{1,0:T(8,128)}, f32[128,2048]{1,0:T(8,128)}), (f32[128,2048]{1,0:T(8,128)}, f32[128,2048]{1,0:T(8,128)})) %all-reduce.23.cloned.1.call-update) | async-done | bytes 2097168 | tf_op jit(solution)/shard_map/psum | solution.py:111
  883.4 53.5 %all_to_all.183 = f32[8,1,128,512]{3,2,1,0:T(8,128)} all-to-all(f32[8,1,128,512]{3,2,1,0:T(8,128)S(1)} %broadcast_in_dim.22), channel_id=1, replica_groups=mesh['row'=4,'col'=8] {'col'}, dimensions={0} | all-to-all | bytes 4194304 | tf_op jit(solution)/shard_map/all_to_all | solution.py:21
  941.9 37.2 %fusion.3 = f32[128,4096]{1,0:T(8,128)S(1)} fusion(f32[4096,2048]{1,0:T(8,128)} %param.5, f32[128,2048]{1,0:T(8,128)S(1)} %get-tuple-element.12), kind=kOutput, calls=%fused_computation.23 | convolution fusion | flops 12885426176 | bytes 36700160 | tf_op jit(solution)/shard_map/dot_general | solution.py:90
  982.0 64.7 %all-reduce.19.cloned.1.call-done = f32[128,2,2048]{2,1,0:T(2,128)} async-done(((f32[128,2,2048]{2,1,0:T(2,128)}), f32[128,2,2048]{2,1,0:T(2,128)}) %all-reduce.19.cloned.1.call-update) | async-done | bytes 2097168 | tf_op jit(solution)/shard_map/psum | solution.py:100
  1054.7 22.4 %fusion.19 = f32[128,2048]{1,0:T(8,128)} fusion(f32[128,4096]{0,1:T(8,128)S(1)} %bitcast.98, f32[4096,2048]{1,0:T(8,128)} %param.5), kind=kOutput, calls=%fused_computation.51 | convolution fusion | flops 12884901888 | bytes 36700160 | tf_op jit(solution)/shard_map/dot_general | solution.py:108
  1104.3 24.7 %all-gather.7 = f32[8,1,128]{2,1,0:T(1,128)S(1)} all-gather(f32[1,1,128]{2,1,0:T(1,128)S(1)} %bitcast.112), channel_id=5, replica_groups=mesh['row'=4,'col'=8] {'col'}, dimensions={0}, use_global_device_ids=true | all-gather | bytes 4608 | tf_op jit(solution)/shard_map/all_gather | solution.py:97
  1131.9 37.1 %all-reduce.21.cloned.1.call-done = (f32[128,2048]{1,0:T(8,128)}, f32[128,2048]{1,0:T(8,128)}) async-done(((f32[128,2048]{1,0:T(8,128)}, f32[128,2048]{1,0:T(8,128)}), (f32[128,2048]{1,0:T(8,128)}, f32[128,2048]{1,0:T(8,128)})) %all-reduce.21.cloned.1.call-update) | async-done | bytes 2097168 | tf_op jit(solution)/shard_map/psum | solution.py:111
  (110 shorter events, 206.3 us)
Async XLA Ops:
  65.5 110.4 %all-to-all-start.1 = ((f32[1,8,128,512]{3,2,0,1:T(8,128)}), f32[1,8,128,512]{3,2,0,1:T(8,128)}, u32[]{:S(2)}, u32[]{:S(2)}) async-start(f32[1,8,128,512]{3,2,0,1:T(8,128)} %bitcast.1), calls=%async_computation.1 | async-start | bytes 4194304 | tf_op jit(solution)/shard_map/all_to_all | solution.py:20
  70.1 104.8 %all-reduce.13.cloned.1.call-start = ((), (), s32[]{:S(2)}) async-start(), calls=%async_computation.16 | async-start | bytes 4194304 | tf_op jit(solution)/shard_map/psum | solution.py:100
  177.2 51.3 %all-to-all-start.2 = ((f32[4,2,128,256]{3,1,2,0:T(2,128)}), f32[4,2,128,256]{3,1,2,0:T(2,128)}, u32[]{:S(2)}, u32[]{:S(2)}) async-start(f32[4,2,128,256]{3,1,2,0:T(2,128)} %broadcast_in_dim.17), calls=%async_computation.2 | async-start | bytes 2097152 | tf_op jit(solution)/shard_map/all_to_all | solution.py:42
  181.4 116.4 %all-reduce.27.cloned.1.call-start = ((), (), s32[]{:S(2)}) async-start(), calls=%async_computation.23 | async-start | bytes 4194304 | tf_op jit(solution)/shard_map/psum | solution.py:111
  230.8 30.1 %all-to-all-start.3 = ((f32[1,8,128,256]{3,2,0,1:T(8,128)}), f32[1,8,128,256]{3,2,0,1:T(8,128)S(1)}, u32[]{:S(2)}, u32[]{:S(2)}) async-start(f32[1,8,128,256]{3,2,0,1:T(8,128)} %bitcast.7), calls=%async_computation.3 | async-start | bytes 2097152 | tf_op jit(solution)/shard_map/all_to_all | solution.py:41
  354.8 113.3 %all-to-all-start.5 = ((f32[1,8,128,512]{3,2,0,1:T(8,128)}), f32[1,8,128,512]{3,2,0,1:T(8,128)}, u32[]{:S(2)}, u32[]{:S(2)}) async-start(f32[1,8,128,512]{3,2,0,1:T(8,128)} %bitcast.100), calls=%async_computation.5 | async-start | bytes 4194304 | tf_op jit(solution)/shard_map/all_to_all | solution.py:20
  359.2 107.9 %all-reduce.15.cloned.1.call-start = ((), (), s32[]{:S(2)}) async-start(), calls=%async_computation.17 | async-start | bytes 4194304 | tf_op jit(solution)/shard_map/psum | solution.py:100
  469.3 51.5 %all-to-all-start.6 = ((f32[4,2,128,256]{3,1,2,0:T(2,128)}), f32[4,2,128,256]{3,1,2,0:T(2,128)}, u32[]{:S(2)}, u32[]{:S(2)}) async-start(f32[4,2,128,256]{3,1,2,0:T(2,128)} %broadcast_in_dim.19), calls=%async_computation.6 | async-start | bytes 2097152 | tf_op jit(solution)/shard_map/all_to_all | solution.py:42
  473.6 116.6 %all-reduce.25.cloned.1.call-start = ((), (), s32[]{:S(2)}) async-start(), calls=%async_computation.22 | async-start | bytes 4194304 | tf_op jit(solution)/shard_map/psum | solution.py:111
  523.2 67.0 %copy-start.1 = (f32[128,2048]{1,0:T(8,128)S(1)}, f32[128,2048]{1,0:T(8,128)}, u32[]{:S(2)}) copy-start(f32[128,2048]{1,0:T(8,128)} %copy-done) | copy-start | bytes 3145732
  523.2 30.2 %all-to-all-start.7 = ((f32[1,8,128,256]{3,2,0,1:T(8,128)}), f32[1,8,128,256]{3,2,0,1:T(8,128)S(1)}, u32[]{:S(2)}, u32[]{:S(2)}) async-start(f32[1,8,128,256]{3,2,0,1:T(8,128)} %bitcast.106), calls=%async_computation.7 | async-start | bytes 2097152 | tf_op jit(solution)/shard_map/all_to_all | solution.py:41
  647.4 110.5 %all-to-all-start.9 = ((f32[1,8,128,512]{3,2,0,1:T(8,128)}), f32[1,8,128,512]{3,2,0,1:T(8,128)}, u32[]{:S(2)}, u32[]{:S(2)}) async-start(f32[1,8,128,512]{3,2,0,1:T(8,128)} %bitcast.23), calls=%async_computation.9 | async-start | bytes 4194304 | tf_op jit(solution)/shard_map/all_to_all | solution.py:20
  651.8 105.0 %all-reduce.17.cloned.1.call-start = ((), (), s32[]{:S(2)}) async-start(), calls=%async_computation.18 | async-start | bytes 4194304 | tf_op jit(solution)/shard_map/psum | solution.py:100
  759.1 51.3 %all-to-all-start.10 = ((f32[4,2,128,256]{3,1,2,0:T(2,128)}), f32[4,2,128,256]{3,1,2,0:T(2,128)}, u32[]{:S(2)}, u32[]{:S(2)}) async-start(f32[4,2,128,256]{3,1,2,0:T(2,128)} %broadcast_in_dim.21), calls=%async_computation.10 | async-start | bytes 2097152 | tf_op jit(solution)/shard_map/all_to_all | solution.py:42
  763.4 116.4 %all-reduce.23.cloned.1.call-start = ((), (), s32[]{:S(2)}) async-start(), calls=%async_computation.21 | async-start | bytes 4194304 | tf_op jit(solution)/shard_map/psum | solution.py:111
  812.8 67.0 %copy-start.6 = (f32[128,2048]{1,0:T(8,128)S(1)}, f32[128,2048]{1,0:T(8,128)}, u32[]{:S(2)}) copy-start(f32[128,2048]{1,0:T(8,128)} %copy-done.5) | copy-start | bytes 3145732
  812.8 30.2 %all-to-all-start.11 = ((f32[1,8,128,256]{3,2,0,1:T(8,128)}), f32[1,8,128,256]{3,2,0,1:T(8,128)S(1)}, u32[]{:S(2)}, u32[]{:S(2)}) async-start(f32[1,8,128,256]{3,2,0,1:T(8,128)} %bitcast.107), calls=%async_computation.11 | async-start | bytes 2097152 | tf_op jit(solution)/shard_map/all_to_all | solution.py:41
  936.9 110.7 %all-to-all-start.13 = ((f32[1,8,128,512]{3,2,0,1:T(8,128)}), f32[1,8,128,512]{3,2,0,1:T(8,128)}, u32[]{:S(2)}, u32[]{:S(2)}) async-start(f32[1,8,128,512]{3,2,0,1:T(8,128)} %bitcast.34), calls=%async_computation.13 | async-start | bytes 4194304 | tf_op jit(solution)/shard_map/all_to_all | solution.py:20
  941.4 105.3 %all-reduce.19.cloned.1.call-start = ((), (), s32[]{:S(2)}) async-start(), calls=%async_computation.19 | async-start | bytes 4194304 | tf_op jit(solution)/shard_map/psum | solution.py:100
  1048.9 50.7 %all-to-all-start.14 = ((f32[4,2,128,256]{3,1,2,0:T(2,128)}), f32[4,2,128,256]{3,1,2,0:T(2,128)S(1)}, u32[]{:S(2)}, u32[]{:S(2)}) async-start(f32[4,2,128,256]{3,1,2,0:T(2,128)} %broadcast_in_dim.23), calls=%async_computation.14 | async-start | bytes 2097152 | tf_op jit(solution)/shard_map/all_to_all | solution.py:42
  1052.6 116.5 %all-reduce.21.cloned.1.call-start = ((), (), s32[]{:S(2)}) async-start(), calls=%async_computation.20 | async-start | bytes 4194304 | tf_op jit(solution)/shard_map/psum | solution.py:111
  1100.6 68.4 %copy-start.3 = (f32[128,2048]{1,0:T(8,128)S(1)}, f32[128,2048]{1,0:T(8,128)}, u32[]{:S(2)}) copy-start(f32[128,2048]{1,0:T(8,128)} %copy-done.2) | copy-start | bytes 3145732
  1100.6 68.4 %copy-start.8 = (f32[128,2048]{1,0:T(8,128)S(1)}, f32[128,2048]{1,0:T(8,128)}, u32[]{:S(2)}) copy-start(f32[128,2048]{1,0:T(8,128)} %copy-done.7) | copy-start | bytes 3145732
  1100.7 30.2 %all-to-all-start.15 = ((f32[1,8,128,256]{3,2,0,1:T(8,128)}), f32[1,8,128,256]{3,2,0,1:T(8,128)S(1)}, u32[]{:S(2)}, u32[]{:S(2)}) async-start(f32[1,8,128,256]{3,2,0,1:T(8,128)} %bitcast.105), calls=%async_computation.15 | async-start | bytes 2097152 | tf_op jit(solution)/shard_map/all_to_all | solution.py:41
  (5 other events, 124.7 us)
Sparse Core Ops, SparseCore 0:
  110.4 64.4 all-reduce.12
  402.6 64.4 all-reduce.14
  692.3 64.4 all-reduce.16
  982.1 64.5 all-reduce.18
Sparse Core Ops, SparseCore 1:
  228.5 69.2 all-reduce.26
  521.0 69.2 all-reduce.24
  810.5 69.2 all-reduce.22
  1099.6 69.3 all-reduce.20
